TPU v7x, 32 devices: a whole 2x2x4 slice. The times are simulated.
32 devices in a mesh: curve: 8 (over y, x, core), sub: 4 (over z).
Axes of the slice: x: 2, y: 2, z: 4, core: 2. Of those that a mesh axis runs over, the one named last changes fastest.
Arguments:
- populations: float32 [19, 2048, 256], P(None, ('curve', 'sub')), may hold values from 0.2 to 1.8
- count_old: int32 [8, 4], replicated, may hold values from 2 to 4, as said below
- count_new: int32 [8, 4], replicated, may hold values from 2 to 4, as said below
Outputs:
- evolved: float32 [19, 2048, 256], P(None, ('curve', 'sub'))
Inputs may be any that keep to these rules, and one draw needn't show every extreme that they name: Each row of count_old sums to 3 times the number of devices along sub, so the blocks of a curve segment stay within it; every row has an entry 4. Each row of count_new sums to 3 times the number of devices along sub and has an entry 4. Between count_old and count_new each boundary between the runs of two neighbouring devices moves by at most one block, and in every row one boundary moves, so every block's new owner is its old owner or the device beside it on sub.
All inputs are finite; a program needn't handle non-finite values.
Results may differ from a plain program's by a relative error of at most 0.00002.
Values sent between devices are 32-bit elements; how exact they have to be, the bound alone decides.
No kernel may reach another device: no remote copies, remote signals or barrier semaphores. Data moves between devices by JAX's collectives and lax.ppermute only.
A program may use at most 64 MiB of HBM per device.

v0:
```python
import jax
import jax.numpy as jnp
import numpy as np
from jax import lax
from jax.sharding import PartitionSpec as P

BX = 16
BZ = 16
STEPS = 4


VELOCITY = np.array(
    [
        [0, 0, 0],
        [1, 0, 0],
        [1, 1, 0],
        [1, -1, 0],
        [1, 0, 1],
        [1, 0, -1],
        [-1, 0, 0],
        [-1, 1, 0],
        [-1, -1, 0],
        [-1, 0, 1],
        [-1, 0, -1],
        [0, 1, 0],
        [0, -1, 0],
        [0, 0, 1],
        [0, 0, -1],
        [0, 1, 1],
        [0, 1, -1],
        [0, -1, 1],
        [0, -1, -1],
    ]
)
WEIGHTS = np.array(
    [1.0 / 3.0]
    + [1.0 / 18.0, 1.0 / 36.0, 1.0 / 36.0, 1.0 / 36.0, 1.0 / 36.0] * 2
    + [1.0 / 18.0] * 4
    + [1.0 / 36.0] * 4
)
tau_base = 0.6
smagorinsky = 0.17


def from_behind(value, axis, steps):
    count = lax.axis_size(axis)
    leading, last = (max(0, -steps), min(count, count - steps))
    return lax.ppermute(value, axis, [(source, source + steps) for source in range(leading, last)])


def from_behind_2(value, axis, steps):
    count = lax.axis_size(axis)
    pairs = [(source, (source + steps) % count) for source in range(count)]
    return lax.ppermute(value, axis, pairs)


def collide(lattice):
    weighted = [float(WEIGHTS[direction]) * lattice[direction] for direction in range(19)]
    density = weighted[0]
    for direction in range(1, 19):
        density = density + weighted[direction]
    velocity = []
    for component in range(3):
        moment = jnp.zeros_like(density)
        for direction in range(19):
            factor = int(VELOCITY[direction, component])
            if factor != 0:
                moment = moment + factor * weighted[direction]
        velocity.append(moment / density)
    speed_square = velocity[0] * velocity[0] + velocity[1] * velocity[1] + velocity[2] * velocity[2]
    departure = []
    for direction in range(19):
        along = jnp.zeros_like(density)
        for component in range(3):
            factor = int(VELOCITY[direction, component])
            if factor != 0:
                along = along + factor * velocity[component]
        balance = density * (1.0 + 3.0 * along + 4.5 * along * along - 1.5 * speed_square)
        departure.append(lattice[direction] - balance)
    pairs = [(0, 0), (1, 1), (2, 2), (0, 1), (0, 2), (1, 2)]
    stress = []
    for first_axis, second_axis in pairs:
        total = jnp.zeros_like(density)
        for direction in range(19):
            factor = int(VELOCITY[direction, first_axis]) * int(VELOCITY[direction, second_axis])
            if factor != 0:
                total = total + factor * float(WEIGHTS[direction]) * departure[direction]
        stress.append(total)
    magnitude = jnp.sqrt(
        stress[0] * stress[0]
        + stress[1] * stress[1]
        + stress[2] * stress[2]
        + 2.0 * (stress[3] * stress[3] + stress[4] * stress[4] + stress[5] * stress[5])
    )
    relax_time = 0.5 * (
        tau_base
        + jnp.sqrt(
            tau_base * tau_base
            + 18.0 * np.sqrt(2.0) * smagorinsky * smagorinsky * magnitude / density
        )
    )
    return jnp.stack(
        [lattice[direction] - departure[direction] / relax_time for direction in range(19)]
    )


def roll_cross(plane_set, step_y, step_z):
    moved = jnp.roll(plane_set, step_y * BZ, axis=-1)
    if step_z == 0:
        return moved
    position = jnp.arange(plane_set.shape[-1], dtype=jnp.int32) % BZ
    inner = jnp.roll(moved, step_z, axis=-1)
    outer = jnp.roll(moved, step_z - step_z * BZ, axis=-1)
    border = 0 if step_z > 0 else BZ - 1
    return jnp.where(position == border, outer, inner)


def cross_moves(shifted):
    return jnp.stack(
        [
            roll_cross(shifted[direction], int(VELOCITY[direction, 1]), int(VELOCITY[direction, 2]))
            for direction in range(19)
        ]
    )


def shards(populations, count_old, count_new):
    curve_pos = lax.axis_index("curve")
    sub_pos = lax.axis_index("sub")
    slot_count = populations.shape[1] // BX
    old_row = lax.dynamic_index_in_dim(count_old, curve_pos, 0, keepdims=False)
    new_row = lax.dynamic_index_in_dim(count_new, curve_pos, 0, keepdims=False)
    old_ends = jnp.cumsum(old_row)
    old_starts = old_ends - old_row
    new_ends = jnp.cumsum(new_row)
    new_starts = new_ends - new_row
    held_old = old_row[sub_pos]
    held_new = new_row[sub_pos]
    plane_ids = jnp.arange(slot_count * BX, dtype=jnp.int32)
    live_plane = plane_ids // BX < held_new
    last_block = lax.dynamic_slice_in_dim(populations, (held_old - 1) * BX, BX, 1)
    first_block = populations[:, :BX]
    from_left = from_behind(last_block, "sub", 1)
    from_right = from_behind(first_block, "sub", -1)
    strip = jnp.concatenate([from_left, populations, jnp.zeros_like(first_block)], axis=1)
    strip = lax.dynamic_update_slice_in_dim(strip, from_right, (held_old + 1) * BX, 1)
    offset = new_starts[sub_pos] - old_starts[sub_pos]
    placed = lax.dynamic_slice_in_dim(strip, (offset + 1) * BX, slot_count * BX, 1)
    lattice = jnp.where(live_plane[None, :, None], placed, jnp.ones_like(placed))
    live_end = held_new * BX
    upper_rim = lax.dynamic_slice_in_dim(lattice, live_end - STEPS, STEPS, 1)
    lower_rim = lattice[:, :STEPS]
    below_rim = from_behind_2(upper_rim, ("curve", "sub"), 1)
    above_rim = from_behind_2(lower_rim, ("curve", "sub"), -1)
    widened = jnp.concatenate([below_rim, lattice, jnp.ones_like(lower_rim)], axis=1)
    widened = lax.dynamic_update_slice_in_dim(widened, above_rim, STEPS + live_end, 1)
    for step_index in range(STEPS):
        relaxed = collide(widened)
        shifted = jnp.stack(
            [
                jnp.roll(relaxed[direction], int(VELOCITY[direction, 0]), axis=0)
                for direction in range(19)
            ]
        )
        widened = cross_moves(shifted)
    lattice = widened[:, STEPS : STEPS + slot_count * BX]
    return jnp.where(live_plane[None, :, None], lattice, jnp.zeros_like(lattice))


def solution(mesh):
    in_specs = (P(None, ("curve", "sub"), None), P(), P())
    out_specs = P(None, ("curve", "sub"), None)
    return jax.shard_map(shards, mesh=mesh, in_specs=in_specs, out_specs=out_specs, check_vma=False)
```

profile of v0, /device:TPU:0, one launch (start us, length us, event | category | flops | bytes accessed | tf_op | source)
XLA Modules:
  0.0 63.0 jit_solution(16206610533214813256)
XLA Ops:
  0.0 1.4 %dynamic_slice.29 = s32[1,1]{0,1:T(1,128)} dynamic-slice(s32[8,4]{0,1:T(4,128)} %param.4, s32[]{:T(128)S(6)} %select_n.984, s32[]{:T(128)S(6)} %select_n.986), dynamic_slice_sizes={1,1} | dynamic-slice | bytes 12 | tf_op jit(solution)/shard_map/dynamic_slice | solution.py:137
  2.0 1.1 %fusion.908 = (f32[19,16,256]{2,1,0:T(8,128)S(1)}, f32[19,16,256]{2,1,0:T(8,128)S(1)}) fusion(f32[19,64,256]{2,1,0:T(8,128)} %param.3, s32[]{:T(128)S(6)} %select_n.987), kind=kLoop, calls=%fused_computation.1585 | loop fusion | bytes 1245188 | tf_op jit(solution)/shard_map/slice | solution.py:142
  3.1 5.0 %collective-permute-start = (f32[19,16,256]{2,1,0:T(8,128)S(1)}, f32[19,16,256]{2,1,0:T(8,128)S(1)}, u32[]{:S(2)}, u32[]{:S(2)}) collective-permute-start(f32[19,16,256]{2,1,0:T(8,128)S(1)} %get-tuple-element.100), channel_id=1, source_target_pairs={{0,1},{1,2},{2,3},{4,5},{5,6},{6,7},{8,9},{9,10},{10,11},{12,13},{... | collective-permute-start | bytes 933896 | tf_op jit(solution)/shard_map/ppermute | solution.py:48
  8.1 1.3 %collective-permute-start.1 = (f32[19,16,256]{2,1,0:T(8,128)S(1)}, f32[19,16,256]{2,1,0:T(8,128)S(1)}, u32[]{:S(2)}, u32[]{:S(2)}) collective-permute-start(f32[19,16,256]{2,1,0:T(8,128)S(1)} %get-tuple-element.99), channel_id=1, source_target_pairs={{1,0},{2,1},{3,2},{5,4},{6,5},{7,6},{9,8},{10,9},{11,10},{13,12},{... | collective-permute-start | bytes 933896 | tf_op jit(solution)/shard_map/ppermute | solution.py:48
  9.4 0.9 %dynamic-slice_reduce_fusion = (s32[4]{0:T(128)S(1)}, s32[4]{0:T(128)S(1)}) fusion(s32[8,4]{0,1:T(4,128)} %param.4, s32[]{:T(128)S(6)} %select_n.983, s32[8,4]{0,1:T(4,128)} %param.5), kind=kLoop, calls=%fused_computation.1496 | loop fusion | bytes 68 | tf_op jit(solution)/shard_map/jit(dynamic_index_in_dim)/dynamic_slice | solution.py:131
  10.3 1.3 %dynamic_slice.28 = s32[1,1]{0,1:T(1,128)} dynamic-slice(s32[8,4]{0,1:T(4,128)} %param.5, s32[]{:T(128)S(6)} %select_n.984, s32[]{:T(128)S(6)} %select_n.986), dynamic_slice_sizes={1,1} | dynamic-slice | bytes 12 | tf_op jit(solution)/shard_map/dynamic_slice | solution.py:138
  11.6 0.2 reduce-window.18
  11.8 0.2 reduce-window.19
  12.0 0.6 fusion.891
  13.2 0.6 dynamic_slice.32
  13.8 0.6 %dynamic_slice.34 = s32[1]{0:T(128)} dynamic-slice(s32[4]{0:T(128)S(1)} %bitcast_subtract_fusion.23, s32[]{:T(128)S(6)} %select_n.985), dynamic_slice_sizes={1} | dynamic-slice | bytes 12 | tf_op jit(solution)/shard_map/dynamic_slice | solution.py:147
  16.5 0.3 maximum_maximum_fusion
  16.8 2.1 %collective-permute-done.1 = f32[19,16,256]{2,1,0:T(8,128)S(1)} collective-permute-done((f32[19,16,256]{2,1,0:T(8,128)S(1)}, f32[19,16,256]{2,1,0:T(8,128)S(1)}, u32[]{:S(2)}, u32[]{:S(2)}) %collective-permute-start.1) | collective-permute-done | bytes 311328 | tf_op jit(solution)/shard_map/ppermute | solution.py:48
  18.9 0.2 dynamic-slice_select_fusion
  19.1 1.6 %collective-permute-start.2 = (f32[19,4,256]{2,1,0:T(4,128)S(1)}, f32[19,4,256]{2,1,0:T(4,128)S(1)}, u32[]{:S(2)}, u32[]{:S(2)}) collective-permute-start(f32[19,4,256]{2,1,0:T(4,128)S(1)} %get-tuple-element.98), channel_id=1, source_target_pairs={{0,1},{1,2},{2,3},{3,4},{4,5},{5,6},{6,7},{7,8},{8,9},{9,10},{10,1... | collective-permute-start | bytes 233480 | tf_op jit(solution)/shard_map/ppermute | solution.py:54
  20.7 3.8 %collective-permute-start.3 = (f32[19,4,256]{2,1,0:T(4,128)S(1)}, f32[19,4,256]{2,1,0:T(4,128)S(1)}, u32[]{:S(2)}, u32[]{:S(2)}) collective-permute-start(f32[19,4,256]{2,1,0:T(4,128)S(1)} %get-tuple-element.97), channel_id=1, source_target_pairs={{0,31},{1,0},{2,1},{3,2},{4,3},{5,4},{6,5},{7,6},{8,7},{9,8},{10,9... | collective-permute-start | bytes 233480 | tf_op jit(solution)/shard_map/ppermute | solution.py:54
  24.5 2.6 %collective-permute-done.2 = f32[19,4,256]{2,1,0:T(4,128)S(1)} collective-permute-done((f32[19,4,256]{2,1,0:T(4,128)S(1)}, f32[19,4,256]{2,1,0:T(4,128)S(1)}, u32[]{:S(2)}, u32[]{:S(2)}) %collective-permute-start.2) | collective-permute-done | bytes 77856 | tf_op jit(solution)/shard_map/ppermute | solution.py:54
  27.1 0.2 maximum_maximum_fusion.1
  27.3 0.2 fusion.103
  27.6 0.6 bitcast_subtract_fusion.19
  28.3 0.2 bitcast_subtract_fusion.4
  28.7 0.1 bitcast_subtract_fusion.1
  29.7 0.1 pad_maximum_fusion.29
  29.8 0.1 slice_maximum_fusion.17
  30.7 0.1 pad_maximum_fusion.28
  31.5 0.1 pad_maximum_fusion.26
  32.1 0.1 slice_maximum_fusion.15
  32.2 1.3 %divide_subtract_fusion.53 = (f32[72,256]{1,0:T(8,128)S(1)}, f32[72,256]{1,0:T(8,128)S(1)}, f32[72,256]{1,0:T(8,128)S(1)}, f32[72,256]{1,0:T(8,128)S(1)}, f32[72...) fusion(f32[72,240]{1,0:T(8,128)S(1)} %pad_maximum_fusion.33, ...), kind=kLoop, calls=%fused_computation.1311 | loop fusion | flops 6746112 | bytes 3686912 | tf_op jit(solution)/shard_map/sub | solution.py:103
  33.6 0.3 divide_subtract_fusion.38
  34.1 0.3 divide_subtract_fusion.45
  35.3 0.1 pad_maximum_fusion.21
  35.4 0.1 slice_maximum_fusion.11
  36.3 0.1 pad_maximum_fusion.20
  37.2 0.1 pad_maximum_fusion.18
  37.8 0.1 slice_maximum_fusion.9
  37.9 1.3 %divide_subtract_fusion.35 = (f32[72,256]{1,0:T(8,128)S(1)}, f32[72,256]{1,0:T(8,128)S(1)}, f32[72,256]{1,0:T(8,128)S(1)}, f32[72,256]{1,0:T(8,128)S(1)}, f32[72...) fusion(f32[71,256]{1,0:T(8,128)S(1)} %get-tuple-element.262, ...), kind=kLoop, calls=%fused_computation.1243 | loop fusion | flops 6746112 | bytes 3686912 | tf_op jit(solution)/shard_map/sub | solution.py:103
  39.2 0.3 divide_subtract_fusion.26
  39.9 0.1 slice_maximum_fusion.3
  40.1 0.1 pad_maximum_fusion.12
  40.6 0.1 pad_maximum_fusion.13
  40.7 0.1 slice_maximum_fusion.5
  40.8 0.2 divide_subtract_fusion.28
  42.5 0.1 pad_maximum_fusion.10
  46.5 1.3 %divide_subtract_fusion = (f32[72,256]{1,0:T(8,128)S(1)}, f32[72,256]{1,0:T(8,128)S(1)}, f32[72,256]{1,0:T(8,128)S(1)}, f32[72,256]{1,0:T(8,128)S(1)}, f32[72,25...) fusion(f32[72,16]{1,0:T(8,128)S(1)} %get-tuple-element.205, ...), kind=kLoop, calls=%fused_computation.1157 | loop fusion | flops 6746112 | bytes 3539456 | tf_op jit(solution)/shard_map/sub | solution.py:103
  47.8 0.2 divide_subtract_fusion.10
  48.1 0.5 divide_subtract_fusion.1
  50.1 0.1 maximum_bitcast_fusion.3
  50.6 0.1 maximum_bitcast_fusion.2
  50.7 0.1 fusion.656
  51.0 0.1 maximum_bitcast_fusion.1
  51.5 0.1 maximum_bitcast_fusion
  51.6 0.1 fusion.654
  51.9 8.0 %subtract_dynamic-update-slice_fusion = f32[19,72,256]{2,1,0:T(8,128)S(1)} fusion(f32[1,72,255]{2,1,0:T(8,128)S(1)} %bitcast.919, f32[1,72,1]{2,1,0:T(8,128)S(1)} %get-tuple-element.174, f32[1,72,15]{2,1,0:T(8,128)S(1)} %get-tuple-element.172, f32[1,72,241]{2,1,0:T(8,128)S(1)} %bitcast.920, f32[1,72,1]{2,1,0:T(8,128)S(1)} %get-tuple-element.178, ...), kind=kLoop, calls=%fused_computation.1184 | loop fusion | flops 26136576 | bytes 7668224
  60.2 0.1 fusion.673
  60.4 0.1 fusion.674
  60.7 0.1 fusion.676
  60.8 0.1 fusion.677
  61.1 0.1 fusion.680
  61.2 0.1 fusion.681
  61.3 0.1 fusion.682
  61.4 0.1 fusion.683
  61.5 0.1 fusion.684
  61.6 0.1 fusion.685
  61.7 1.3 %slice_select_fusion = f32[19,64,256]{2,1,0:T(8,128)} fusion(f32[19,72,256]{2,1,0:T(8,128)S(1)} %fusion.685, pred[64]{0:T(512)(128)(4,1)S(1)} %fusion.891), kind=kLoop, calls=%fused_computation.2 | loop fusion | flops 311296 | bytes 2490432 | tf_op jit(solution)/shard_map/jit(_where)/select_n | solution.py:167
  (351 shorter events, 14.8 us)
Async XLA Ops:
  0.0 16.5 %copy-start = (f32[19,64,256]{2,1,0:T(8,128)S(1)}, f32[19,64,256]{2,1,0:T(8,128)}, u32[]{:S(2)}) copy-start(f32[19,64,256]{2,1,0:T(8,128)} %param.3) | copy-start | bytes 3735556
  3.1 13.4 %collective-permute-start = (f32[19,16,256]{2,1,0:T(8,128)S(1)}, f32[19,16,256]{2,1,0:T(8,128)S(1)}, u32[]{:S(2)}, u32[]{:S(2)}) collective-permute-start(f32[19,16,256]{2,1,0:T(8,128)S(1)} %get-tuple-element.100), channel_id=1, source_target_pairs={{0,1},{1,2},{2,3},{4,5},{5,6},{6,7},{8,9},{9,10},{10,11},{12,13},{... | collective-permute-start | bytes 933896 | tf_op jit(solution)/shard_map/ppermute | solution.py:48
  8.1 10.7 %collective-permute-start.1 = (f32[19,16,256]{2,1,0:T(8,128)S(1)}, f32[19,16,256]{2,1,0:T(8,128)S(1)}, u32[]{:S(2)}, u32[]{:S(2)}) collective-permute-start(f32[19,16,256]{2,1,0:T(8,128)S(1)} %get-tuple-element.99), channel_id=1, source_target_pairs={{1,0},{2,1},{3,2},{5,4},{6,5},{7,6},{9,8},{10,9},{11,10},{13,12},{... | collective-permute-start | bytes 933896 | tf_op jit(solution)/shard_map/ppermute | solution.py:48
  19.1 8.0 %collective-permute-start.2 = (f32[19,4,256]{2,1,0:T(4,128)S(1)}, f32[19,4,256]{2,1,0:T(4,128)S(1)}, u32[]{:S(2)}, u32[]{:S(2)}) collective-permute-start(f32[19,4,256]{2,1,0:T(4,128)S(1)} %get-tuple-element.98), channel_id=1, source_target_pairs={{0,1},{1,2},{2,3},{3,4},{4,5},{5,6},{6,7},{7,8},{8,9},{9,10},{10,1... | collective-permute-start | bytes 233480 | tf_op jit(solution)/shard_map/ppermute | solution.py:54
  20.7 6.5 %collective-permute-start.3 = (f32[19,4,256]{2,1,0:T(4,128)S(1)}, f32[19,4,256]{2,1,0:T(4,128)S(1)}, u32[]{:S(2)}, u32[]{:S(2)}) collective-permute-start(f32[19,4,256]{2,1,0:T(4,128)S(1)} %get-tuple-element.97), channel_id=1, source_target_pairs={{0,31},{1,0},{2,1},{3,2},{4,3},{5,4},{6,5},{7,6},{8,7},{9,8},{10,9... | collective-permute-start | bytes 233480 | tf_op jit(solution)/shard_map/ppermute | solution.py:54
where the time goes:
time: 63.3 us; the launch traced here: 63 us
  other arithmetic  29.2 us (46%)
  local copies, waits for them, and re-layouts  12.4 us (20%)
  starting transfers between devices  11.7 us (18%)
  between operations  5.16 us (8%)
  waiting for transfers between devices  4.61 us (7%)
    unnamed x18, other arithmetic  9.36 us
    sub x12, other arithmetic, collide(): lattice[direction] - departure[direction] / relax_time  6.72 us
    ppermute x2, starting transfers between devices, from_behind(): lax.ppermute(value, axis, [(source, source + steps) for source in range(l...  6.27 us
    ppermute x2, starting transfers between devices, from_behind_2(): return lax.ppermute(value, axis, pairs)  5.4 us
    concatenate x76, other arithmetic, shards(): jnp.roll(relaxed[direction], int(VELOCITY[direction, 0]), axis=0)  3.51 us
    concatenate x48, other arithmetic, roll_cross(): moved = jnp.roll(plane_set, step_y * BZ, axis=-1)  3.3 us
    ppermute x2, waiting for transfers between devices, from_behind_2(): return lax.ppermute(value, axis, pairs)  2.56 us
    ppermute x2, waiting for transfers between devices, from_behind(): lax.ppermute(value, axis, [(source, source + steps) for source in range(l...  2.06 us
  transfers between devices with their start and end apart: 4, of which 2 were waited for; matrix products, arithmetic and copies ran while one was open for 8% of the time, Pallas kernels for 0%

commit v1 on v0

v1 whole, which is shorter than its diff:
```python
import functools

import jax
import jax.numpy as jnp
import numpy as np
from jax import lax
from jax.experimental import pallas as pl
from jax.experimental.pallas import tpu as pltpu
from jax.sharding import PartitionSpec as P

BX = 16
BZ = 16
STEPS = 4
DIRS = 19
REACH = BX + STEPS
LANES = 128
HALVES = 2
HOME = 40
TOP = 8

VELOCITY = np.array(
    [
        [0, 0, 0],
        [1, 0, 0],
        [1, 1, 0],
        [1, -1, 0],
        [1, 0, 1],
        [1, 0, -1],
        [-1, 0, 0],
        [-1, 1, 0],
        [-1, -1, 0],
        [-1, 0, 1],
        [-1, 0, -1],
        [0, 1, 0],
        [0, -1, 0],
        [0, 0, 1],
        [0, 0, -1],
        [0, 1, 1],
        [0, 1, -1],
        [0, -1, 1],
        [0, -1, -1],
    ]
)
tau_base = 0.6
smagorinsky = 0.17


def collide(h):
    def pair(first, second):
        return h[first] + h[second], h[first] - h[second]

    s_x, d_x = pair(1, 6)
    s_xyp, d_xyp = pair(2, 8)
    s_xym, d_xym = pair(3, 7)
    s_xzp, d_xzp = pair(4, 10)
    s_xzm, d_xzm = pair(5, 9)
    s_y, d_y = pair(11, 12)
    s_z, d_z = pair(13, 14)
    s_yzp, d_yzp = pair(15, 18)
    s_yzm, d_yzm = pair(16, 17)
    j_x = (d_x + d_x) + (d_xyp + d_xym) + (d_xzp + d_xzm)
    j_y = (d_y + d_y) + (d_xyp - d_xym) + (d_yzp + d_yzm)
    j_z = (d_z + d_z) + (d_xzp - d_xzm) + (d_yzp - d_yzm)
    t_xy, t_xz, t_yz = s_xyp + s_xym, s_xzp + s_xzm, s_yzp + s_yzm
    m_xy, m_xz, m_yz = s_xyp - s_xym, s_xzp - s_xzm, s_yzp - s_yzm
    ss_x, ss_y, ss_z = s_x + s_x, s_y + s_y, s_z + s_z
    yz_part = ss_y + t_yz
    m_xx = ss_x + (t_xy + t_xz)
    m_yy = yz_part + t_xy
    m_zz = ss_z + (t_xz + t_yz)
    rho36 = (12.0 * h[0] + ss_z) + (m_xx + yz_part)
    inverse = 1.0 / rho36
    k_u = 1.5 * inverse
    k_p = 2.25 * inverse
    u_x, u_y, u_z = j_x * k_u, j_y * k_u, j_z * k_u
    xx, yy, zz = u_x * u_x, u_y * u_y, u_z * u_z
    xy, xz, yz = u_x * u_y, u_x * u_z, u_y * u_z
    p_xx = m_xx * k_p - (xx + 0.75)
    p_yy = m_yy * k_p - (yy + 0.75)
    p_zz = m_zz * k_p - (zz + 0.75)
    p_xy = m_xy * k_p - xy
    p_xz = m_xz * k_p - xz
    p_yz = m_yz * k_p - yz
    off = p_xy * p_xy + p_xz * p_xz + p_yz * p_yz
    square = (p_xx * p_xx + p_yy * p_yy) + (p_zz * p_zz + (off + off))
    magnitude = jnp.sqrt(square)
    factor = 18.0 * np.sqrt(2.0) * smagorinsky * smagorinsky / 2.25
    inner = tau_base * tau_base + float(factor) * magnitude
    omega = 2.0 / (tau_base + inner * lax.rsqrt(inner))
    keep = 1.0 - omega
    gain = (omega * (1.0 / 36.0)) * rho36
    gain2 = gain + gain
    rest = gain - gain * ((2.0 / 3.0) * ((xx + yy) + zz))
    gain4 = gain2 + gain2
    a_x, a_y, a_z = gain2 * u_x, gain2 * u_y, gain2 * u_z
    b_x, b_y, b_z = a_x * u_x, a_y * u_y, a_z * u_z
    n_x, n_y, n_z = rest + b_x, rest + b_y, rest + b_z
    out = [None] * DIRS
    out[0] = keep * h[0] + rest

    def spread(first, second, even, odd):
        out[first] = keep * h[first] + (even + odd)
        out[second] = keep * h[second] + (even - odd)

    spread(1, 6, n_x, a_x)
    spread(11, 12, n_y, a_y)
    spread(13, 14, n_z, a_z)
    for plus, minus, base, cross, first, second in (
        ((2, 8), (3, 7), n_x + b_y, gain4 * xy, a_x, a_y),
        ((4, 10), (5, 9), n_x + b_z, gain4 * xz, a_x, a_z),
        ((15, 18), (16, 17), n_y + b_z, gain4 * yz, a_y, a_z),
    ):
        spread(*plus, base + cross, first + second)
        spread(*minus, base - cross, first - second)
    return out


def lane_sources(step_y, step_z):
    lane = lax.broadcasted_iota(jnp.int32, (8, LANES), 1)
    along_y = (lane - step_y * BZ) & (LANES - 1) & ~(BZ - 1)
    along_z = (lane - step_z) & (BZ - 1)
    return along_y | along_z


def moves():
    lane = lax.broadcasted_iota(jnp.int32, (8, LANES), 1)
    index = {}
    for step_y in (-1, 0, 1):
        for step_z in (-1, 1):
            index[step_y, step_z] = lane_sources(step_y, step_z)
    border = {1: lane < BZ, -1: lane >= LANES - BZ}
    return index, border


def shift_cross(lower, upper, direction, tables):
    index, border = tables
    step_y, step_z = int(VELOCITY[direction, 1]), int(VELOCITY[direction, 2])
    if step_z != 0:
        source = index[step_y, step_z]
        lower = jnp.take_along_axis(lower, source, axis=1, mode="promise_in_bounds")
        upper = jnp.take_along_axis(upper, source, axis=1, mode="promise_in_bounds")
    elif step_y != 0:
        lower = pltpu.roll(lower, (step_y * BZ) % LANES, 1)
        upper = pltpu.roll(upper, (step_y * BZ) % LANES, 1)
    if step_y != 0:
        edge = border[step_y]
        lower, upper = jnp.where(edge, upper, lower), jnp.where(edge, lower, upper)
    return lower, upper


def layout_of(sub_count, old_ref, new_ref, curve, sub):
    old_start, new_start = 0, 0
    for other in range(sub_count - 1):
        before = other < sub
        old_start += jnp.where(before, old_ref[other, curve], 0)
        new_start += jnp.where(before, new_ref[other, curve], 0)
    held_old = old_ref[sub, curve] * BX
    held_new = new_ref[sub, curve] * BX
    return held_old, held_new, (new_start - old_start) * BX


def pack_kernel(sub_count, old_ref, new_ref, pop_ref, one_ref, two_ref, far_ref, all_ref, sem):
    curve, sub = lax.axis_index("curve"), lax.axis_index("sub")
    loads = [
        pltpu.make_async_copy(pop_ref.at[:, :, half * LANES : (half + 1) * LANES], all_ref.at[:, half], sem.at[half])
        for half in range(HALVES)
    ]
    for load in loads:
        load.start()
    held_old, _, _ = layout_of(sub_count, old_ref, new_ref, curve, sub)
    for load in loads:
        load.wait()
    even = sub % 2 == 0
    right = held_old - REACH
    one_start = jnp.where(even, right, 0)
    two_start = jnp.where(even, 0, right)
    far_start = jnp.where(sub == 0, 0, held_old - STEPS)
    for target, start, count in (
        (one_ref, one_start, REACH),
        (two_ref, two_start, REACH),
        (far_ref, far_start, STEPS),
    ):
        for direction in range(DIRS):
            for half in range(HALVES):
                row = (direction * HALVES + half) * count
                target[row : row + count, :] = all_ref[direction, half, pl.ds(start, count), :]


def step_kernel(
    sub_count, slots, old_ref, new_ref, pop_ref, one_ref, two_ref, far_ref, out_ref,
    first_ref, ping_ref, pong_ref, sem,
):
    curve, sub = lax.axis_index("curve"), lax.axis_index("sub")
    held_old, held_new, offset = layout_of(sub_count, old_ref, new_ref, curve, sub)
    home = pl.multiple_of(HOME - offset, 8)
    loads = [
        pltpu.make_async_copy(
            pop_ref.at[:, :, half * LANES : (half + 1) * LANES],
            first_ref.at[:, half, pl.ds(home, slots * BX), :],
            sem.at[half],
        )
        for half in range(HALVES)
    ]
    for load in loads:
        load.start()
    for load in loads:
        load.wait()

    def place(source, count, start):
        for direction in range(DIRS):
            for half in range(HALVES):
                row = (direction * HALVES + half) * count
                first_ref[direction, half, pl.ds(start, count), :] = source[row : row + count, :]

    even = sub % 2 == 0
    left_row, right_row = home - REACH, home + held_old

    @pl.when(even)
    def _():
        place(one_ref, REACH, right_row)

    @pl.when(jnp.logical_not(even))
    def _():
        place(one_ref, REACH, left_row)

    @pl.when(jnp.logical_and(even, sub > 0))
    def _():
        place(two_ref, REACH, left_row)

    @pl.when(jnp.logical_and(jnp.logical_not(even), sub < sub_count - 1))
    def _():
        place(two_ref, REACH, right_row)

    @pl.when(sub == 0)
    def _():
        place(far_ref, STEPS, home - STEPS)

    @pl.when(sub == sub_count - 1)
    def _():
        place(far_ref, STEPS, right_row)

    tables = moves()
    groups = held_new // 8 + 1

    def run(source, target, base, moving):
        def body(group, carry):
            row = base + group * 8
            relaxed = []
            for half in range(HALVES):
                cells = []
                for direction in range(DIRS):
                    at = row - int(VELOCITY[direction, 0]) if moving else row
                    cells.append(source[direction, half, pl.ds(at, 8), :])
                relaxed.append(collide(cells))
            to = pl.multiple_of(TOP + group * 8, 8)
            for direction in range(DIRS):
                lower, upper = shift_cross(relaxed[0][direction], relaxed[1][direction], direction, tables)
                target[direction, 0, pl.ds(to, 8), :] = lower
                target[direction, 1, pl.ds(to, 8), :] = upper
            return carry

        lax.fori_loop(0, groups, body, 0)

    run(first_ref, ping_ref, HOME - STEPS, False)
    run(ping_ref, pong_ref, TOP + 1, True)
    run(pong_ref, ping_ref, TOP + 1, True)
    run(ping_ref, pong_ref, TOP + 1, True)
    live = held_new // 8
    for group in range(slots * BX // 8):

        @pl.when(group < live)
        def _():
            for direction in range(DIRS):
                row = TOP + 1 + group * 8 - int(VELOCITY[direction, 0])
                for half in range(HALVES):
                    out_ref[direction, group * 8 : group * 8 + 8, half * LANES : (half + 1) * LANES] = pong_ref[
                        direction, half, row : row + 8, :
                    ]

        @pl.when(group >= live)
        def _():
            for direction in range(DIRS):
                out_ref[direction, group * 8 : group * 8 + 8, :] = jnp.zeros((8, HALVES * LANES), jnp.float32)


def shards(populations, count_old, count_new):
    curve_count, sub_count = lax.axis_size("curve"), lax.axis_size("sub")
    planes = populations.shape[1]
    slots = planes // BX
    total = curve_count * sub_count
    old, new = count_old.T, count_new.T
    smem = pl.BlockSpec(memory_space=pltpu.SMEM)
    hbm = pl.BlockSpec(memory_space=pl.ANY)
    vmem = pl.BlockSpec(memory_space=pltpu.VMEM)
    rows = DIRS * HALVES
    near = jax.ShapeDtypeStruct((rows * REACH, LANES), jnp.float32)
    far = jax.ShapeDtypeStruct((rows * STEPS, LANES), jnp.float32)
    one, two, rim = pl.pallas_call(
        functools.partial(pack_kernel, sub_count),
        out_shape=(near, near, far),
        in_specs=[smem, smem, hbm],
        out_specs=(vmem, vmem, vmem),
        scratch_shapes=[
            pltpu.VMEM((DIRS, HALVES, planes, LANES), jnp.float32),
            pltpu.SemaphoreType.DMA((HALVES,)),
        ],
        name="pack",
    )(old, new, populations)
    both = ("curve", "sub")
    inside = [(at, at ^ 1) for at in range(total)]
    between, across = [], []
    for at in range(1, total, 2):
        after = (at + 1) % total
        into = across if after % sub_count == 0 else between
        into += [(at, after), (after, at)]
    one = lax.ppermute(one, both, inside)
    two = lax.ppermute(two, both, between)
    rim = lax.ppermute(rim, both, across)
    return pl.pallas_call(
        functools.partial(step_kernel, sub_count, slots),
        out_shape=jax.ShapeDtypeStruct(populations.shape, jnp.float32),
        in_specs=[smem, smem, hbm, vmem, vmem, vmem],
        out_specs=vmem,
        scratch_shapes=[
            pltpu.VMEM((DIRS, HALVES, HOME + planes + BX + REACH + 4, LANES), jnp.float32),
            pltpu.VMEM((DIRS, HALVES, planes + 3 * 8, LANES), jnp.float32),
            pltpu.VMEM((DIRS, HALVES, planes + 3 * 8, LANES), jnp.float32),
            pltpu.SemaphoreType.DMA((HALVES,)),
        ],
        name="steps",
    )(old, new, populations, one, two, rim)


def solution(mesh):
    if mesh.shape["sub"] % 2:
        raise ValueError("odd sub")
    in_specs = (P(None, ("curve", "sub"), None), P(), P())
    out_specs = P(None, ("curve", "sub"), None)
    return jax.shard_map(shards, mesh=mesh, in_specs=in_specs, out_specs=out_specs, check_vma=False)
```

time: 63.3 us -> 31.1 us (0.49)
  other arithmetic: 29.2 us -> 0 us
  Pallas kernels: 0 us -> 12.1 us
  local copies, waits for them, and re-layouts: 12.4 us -> 1.54 us
  between operations: 5.16 us -> 0.03 us
  waiting for transfers between devices: 4.61 us -> 7.73 us
  starting transfers between devices: 11.7 us -> 9.22 us
    pallas_call x0 -> x2, Pallas kernels: none -> 12.1 us  [the longest x1 9.08 us: shards(): pl.pallas_call(functools.partial(step_kernel, sub_count, slots), out_shap...]
    concatenate x186 -> x0, other arithmetic: 10.3 us -> none  [the longest x76 3.51 us: shards(): jnp.roll(relaxed[direction], int(VELOCITY[direction, 0]), axis=0)]
    unnamed x18 -> x0, other arithmetic: 9.36 us -> none
    sub x15 -> x0, other arithmetic: 6.97 us -> none  [the longest x12 6.72 us: collide(): lattice[direction] - departure[direction] / relax_time]
    dynamic_slice x5 -> x0, local copies, waits for them, and re-layouts: 4.82 us -> none  [the longest x1 1.36 us: shards(): held_old = old_row[sub_pos]]
    slice x104 -> x0, local copies, waits for them, and re-layouts: 4.05 us -> none  [the longest x31 1.63 us: roll_cross(): moved = jnp.roll(plane_set, step_y * BZ, axis=-1)]
    concatenate x66 -> x0, local copies, waits for them, and re-layouts: 3.47 us -> none  [the longest x24 1.46 us: roll_cross(): outer = jnp.roll(moved, step_z - step_z * BZ, axis=-1)]
    ppermute x4 -> x3, waiting for transfers between devices: 4.61 us -> 7.73 us  [the longest x1 7.72 us: shards(): rim = lax.ppermute(rim, both, across)]
  transfers between devices with their start and end apart: 4 -> 3, of which waited for: 2 -> 1; matrix products, arithmetic and copies ran while one was open for 8% -> 0% of each run, Pallas kernels for 0% -> 0%
where the time goes in v1:
time: 31.1 us; the launch traced here: 30.6 us
  Pallas kernels  12.1 us (39%)
  starting transfers between devices  9.22 us (30%)
  waiting for transfers between devices  7.73 us (25%)
  local copies, waits for them, and re-layouts  1.54 us (5%)
    pallas_call x1, Pallas kernels, shards(): pl.pallas_call(functools.partial(step_kernel, sub_count, slots), out_shap...  9.08 us
    ppermute x1, waiting for transfers between devices, shards(): rim = lax.ppermute(rim, both, across)  7.72 us
    ppermute x1, starting transfers between devices, shards(): rim = lax.ppermute(rim, both, across)  5.42 us
    ppermute x1, starting transfers between devices, shards(): one = lax.ppermute(one, both, inside)  3.12 us
    pallas_call x1, Pallas kernels, shards(): pl.pallas_call(functools.partial(pack_kernel, sub_count), out_shape=(near...  3 us
    unnamed x6, local copies, waits for them, and re-layouts  1.54 us
    ppermute x1, starting transfers between devices, shards(): two = lax.ppermute(two, both, between)  0.67 us
  transfers between devices with their start and end apart: 3, of which 1 were waited for; matrix products, arithmetic and copies ran while one was open for 0% of the time, Pallas kernels for 0%

profile of v1, /device:TPU:0, one launch (start us, length us, event | category | flops | bytes accessed | tf_op | source)
XLA Modules:
  0.0 30.6 jit_solution(5872747881563244742)
XLA Ops:
  0.0 3.0 %pack.1 = (f32[760,128]{1,0:T(8,128)}, f32[760,128]{1,0:T(8,128)}, f32[152,128]{1,0:T(8,128)}) custom-call(s32[4,8]{1,0:T(4,128)} %bitcast.2, s32[4,8]{1,0:T(4,128)} %bitcast.4, f32[19,64,256]{2,1,0:T(8,128)} %pop_ref.3), custom_call_target="tpu_custom_call" | custom-call | tf_op jit(solution)/shard_map/pack/pallas_call | solution.py:298
  3.0 3.1 %collective-permute-start = (f32[760,128]{1,0:T(8,128)}, f32[760,128]{1,0:T(8,128)S(1)}, u32[]{:S(2)}, u32[]{:S(2)}) collective-permute-start(f32[760,128]{1,0:T(8,128)} %get-tuple-element.8), channel_id=1, source_target_pairs={{0,1},{1,0},{2,3},{3,2},{4,5},{5,4},{6,7},{7,6},{8,9},{9,8},{10,11... | collective-permute-start | bytes 1167368 | tf_op jit(solution)/shard_map/ppermute | solution.py:316
  6.1 0.7 %collective-permute-start.1 = (f32[760,128]{1,0:T(8,128)}, f32[760,128]{1,0:T(8,128)S(1)}, u32[]{:S(2)}, u32[]{:S(2)}) collective-permute-start(f32[760,128]{1,0:T(8,128)} %get-tuple-element.9), channel_id=1, source_target_pairs={{1,2},{2,1},{5,6},{6,5},{9,10},{10,9},{13,14},{14,13},{17,18},{18,... | collective-permute-start | bytes 1167368 | tf_op jit(solution)/shard_map/ppermute | solution.py:317
  6.8 5.4 %collective-permute-start.2 = (f32[152,128]{1,0:T(8,128)}, f32[152,128]{1,0:T(8,128)S(1)}, u32[]{:S(2)}, u32[]{:S(2)}) collective-permute-start(f32[152,128]{1,0:T(8,128)} %get-tuple-element.10), channel_id=1, source_target_pairs={{3,4},{4,3},{7,8},{8,7},{11,12},{12,11},{15,16},{16,15},{19,20},{2... | collective-permute-start | bytes 233480 | tf_op jit(solution)/shard_map/ppermute | solution.py:318
  12.2 7.7 %collective-permute-done.2.far_ref = f32[152,128]{1,0:T(8,128)S(1)} collective-permute-done((f32[152,128]{1,0:T(8,128)}, f32[152,128]{1,0:T(8,128)S(1)}, u32[]{:S(2)}, u32[]{:S(2)}) %collective-permute-start.2) | collective-permute-done | bytes 77856 | tf_op jit(solution)/shard_map/ppermute | solution.py:318
  20.0 0.0 copy-start.2
  20.0 0.0 collective-permute-done.one_ref
  20.0 0.0 copy-start
  20.0 0.0 collective-permute-done.1.two_ref
  20.0 0.6 %copy-done.2 = f32[152,128]{1,0:T(8,128)} copy-done((f32[152,128]{1,0:T(8,128)}, f32[152,128]{1,0:T(8,128)S(1)}, u32[]{:S(2)}) %copy-start.2) | copy-done | bytes 77848
  20.6 0.2 copy-done
  20.8 0.0 copy-start.1
  20.8 0.8 %copy-done.1 = f32[760,128]{1,0:T(8,128)} copy-done((f32[760,128]{1,0:T(8,128)}, f32[760,128]{1,0:T(8,128)S(1)}, u32[]{:S(2)}) %copy-start.1) | copy-done | bytes 389144
  21.5 9.1 %steps.1 = f32[19,64,256]{2,1,0:T(8,128)} custom-call(s32[4,8]{1,0:T(4,128)} %bitcast.3, s32[4,8]{1,0:T(4,128)} %bitcast.5, f32[19,64,256]{2,1,0:T(8,128)} %pop_ref.3, f32[760,128]{1,0:T(8,128)} %copy-done, f32[760,128]{1,0:T(8,128)} %copy-done.1, f32[152,128]{1,0:T(8,128)} %copy-done.2), custom_call_target="tpu_custom_call" | custom-call | tf_op jit(solution)/shard_map/steps/pallas_call | solution.py:319
Async XLA Ops:
  3.0 17.0 %collective-permute-start = (f32[760,128]{1,0:T(8,128)}, f32[760,128]{1,0:T(8,128)S(1)}, u32[]{:S(2)}, u32[]{:S(2)}) collective-permute-start(f32[760,128]{1,0:T(8,128)} %get-tuple-element.8), channel_id=1, source_target_pairs={{0,1},{1,0},{2,3},{3,2},{4,5},{5,4},{6,7},{7,6},{8,9},{9,8},{10,11... | collective-permute-start | bytes 1167368 | tf_op jit(solution)/shard_map/ppermute | solution.py:316
  6.1 13.8 %collective-permute-start.1 = (f32[760,128]{1,0:T(8,128)}, f32[760,128]{1,0:T(8,128)S(1)}, u32[]{:S(2)}, u32[]{:S(2)}) collective-permute-start(f32[760,128]{1,0:T(8,128)} %get-tuple-element.9), channel_id=1, source_target_pairs={{1,2},{2,1},{5,6},{6,5},{9,10},{10,9},{13,14},{14,13},{17,18},{18,... | collective-permute-start | bytes 1167368 | tf_op jit(solution)/shard_map/ppermute | solution.py:317
  6.8 13.2 %collective-permute-start.2 = (f32[152,128]{1,0:T(8,128)}, f32[152,128]{1,0:T(8,128)S(1)}, u32[]{:S(2)}, u32[]{:S(2)}) collective-permute-start(f32[152,128]{1,0:T(8,128)} %get-tuple-element.10), channel_id=1, source_target_pairs={{3,4},{4,3},{7,8},{8,7},{11,12},{12,11},{15,16},{16,15},{19,20},{2... | collective-permute-start | bytes 233480 | tf_op jit(solution)/shard_map/ppermute | solution.py:318
  20.0 0.6 %copy-start.2 = (f32[152,128]{1,0:T(8,128)}, f32[152,128]{1,0:T(8,128)S(1)}, u32[]{:S(2)}) copy-start(f32[152,128]{1,0:T(8,128)S(1)} %collective-permute-done.2.far_ref) | copy-start | bytes 233476
  20.0 0.8 %copy-start = (f32[760,128]{1,0:T(8,128)}, f32[760,128]{1,0:T(8,128)S(1)}, u32[]{:S(2)}) copy-start(f32[760,128]{1,0:T(8,128)S(1)} %collective-permute-done.one_ref) | copy-start | bytes 1167364
  20.8 0.8 %copy-start.1 = (f32[760,128]{1,0:T(8,128)}, f32[760,128]{1,0:T(8,128)S(1)}, u32[]{:S(2)}) copy-start(f32[760,128]{1,0:T(8,128)S(1)} %collective-permute-done.1.two_ref) | copy-start | bytes 1167364
